TPU v7x, 32 devices: a whole 2x2x4 slice. The times are simulated.
32 devices in a mesh: pipe: 8 (over z, core), expert: 4 (over y, x).
Axes of the slice: x: 2, y: 2, z: 4, core: 2. Of those that a mesh axis runs over, the one named last changes fastest.
Arguments:
- acts: bfloat16 [8, 512, 3584], P('pipe', 'expert'), may hold values from -6 to 6
- routing: int32 [8, 512, 8], P('pipe', 'expert'), may hold values from 0 to 255, as said below
- combine_w: float32 [8, 512, 8], P('pipe', 'expert'), may hold values from 0.25 to 2.5
- w_gate_up: bfloat16 [8, 3584, 4096], P('pipe', None, 'expert'), may hold values from -0.09375 to 0.09375
- w_down: bfloat16 [8, 2048, 3584], P('pipe', 'expert'), may hold values from -0.125 to 0.125
Outputs:
- next_acts: bfloat16 [8, 512, 3584], P('pipe', 'expert')
Inputs may be any that keep to these rules, and one draw needn't show every extreme that they name: `routing`: each row names 8 different experts. Within one section every aligned block of 128 rows (the rows of one device) holds the same number of rows naming expert 0, at least 1 and at most 8; in one section of every draw, drawn from the seed, exactly 8.
All inputs are finite; a program needn't handle non-finite values.
Results may differ from a plain program's by a relative error of at most 0.0055.
Values may be sent and summed in bfloat16 or wider, within the bound.
A program may use at most 64 MiB of HBM per device.

v0:
```python
import jax
import jax.numpy as jnp
from jax import lax
from jax.sharding import PartitionSpec as P

CAP = 8


def from_behind(block, axis, distance):
    devices = range(lax.axis_size(axis))
    route = [((i - distance) % len(devices), i) for i in devices]
    return lax.ppermute(block, axis, route)


def per_device(acts, routing, combine_w, w_gate_up, w_down):
    tokens_in = acts[0]
    route_ids = routing[0]
    mix_weights = combine_w[0]
    gate_up_local = w_gate_up[0]
    down_local = w_down[0]
    tok_count = tokens_in.shape[0]
    feature_width = tokens_in.shape[1]
    hid_local = down_local.shape[0]
    devices = lax.axis_size("expert")
    names_zero = route_ids == 0
    chosen = jnp.any(names_zero, axis=1)
    coefficient = jnp.sum(jnp.where(names_zero, mix_weights, 0.0), axis=1)
    position = jnp.cumsum(chosen.astype(jnp.int32)) - 1
    slot_ids = jnp.arange(CAP)
    select = (position[None, :] == slot_ids[:, None]) & chosen[None, :]
    packed = jnp.dot(
        select.astype(jnp.bfloat16), tokens_in, preferred_element_type=jnp.float32
    ).astype(jnp.bfloat16)
    outbound = jnp.broadcast_to(packed[None], (devices, CAP, feature_width))
    rows_in = lax.all_to_all(outbound, "expert", split_axis=0, concat_axis=0, tiled=True)
    flat_rows = rows_in.reshape(-1, feature_width)
    gate_up = jnp.dot(flat_rows, gate_up_local, preferred_element_type=jnp.float32)
    hidden = (jax.nn.silu(gate_up[:, :hid_local]) * gate_up[:, hid_local:]).astype(jnp.bfloat16)
    part_out = jnp.dot(hidden, down_local, preferred_element_type=jnp.float32).astype(jnp.bfloat16)
    partials = part_out.reshape(rows_in.shape)
    returned = lax.all_to_all(partials, "expert", split_axis=0, concat_axis=0, tiled=True)
    merged = jnp.sum(returned, axis=0, dtype=jnp.float32)
    select_table = select.astype(jnp.float32)
    earlier = from_behind(tokens_in, "pipe", 1)
    slot_coeff = jnp.sum(select_table * coefficient[None, :], axis=1)
    compact = slot_coeff[:, None] * merged
    row_index = jnp.arange(tok_count, dtype=jnp.int32)
    where_rows = jnp.sum(select.astype(jnp.int32) * row_index[None, :], axis=1)
    where_rows = where_rows + tok_count * (1 - jnp.any(select, axis=1).astype(jnp.int32))
    got_rows, got_where = (
        from_behind(compact.astype(jnp.bfloat16), "pipe", 1).astype(compact.dtype),
        from_behind(where_rows, "pipe", 1),
    )
    spread = (got_where[None, :] == row_index[:, None]).astype(jnp.float32)
    layer_rows = jnp.dot(spread, got_rows, precision=lax.Precision.HIGHEST)
    arrived = (earlier.astype(jnp.float32) + layer_rows).astype(jnp.bfloat16)
    return arrived[None]


def solution(mesh):
    return jax.shard_map(
        per_device,
        mesh=mesh,
        in_specs=(
            P("pipe", "expert", None),
            P("pipe", "expert", None),
            P("pipe", "expert", None),
            P("pipe", None, "expert"),
            P("pipe", "expert", None),
        ),
        out_specs=P("pipe", "expert", None),
        check_vma=False,
    )
```

profile of v0, /device:TPU:0, one launch (start us, length us, event | category | flops | bytes accessed | tf_op | source)
XLA Modules:
  0.0 35.3 jit_solution(17032349081950597669)
XLA Ops:
  0.0 0.7 %select_reduce_fusion.1 = (f32[128]{0:T(128)S(1)}, pred[1,128,8]{1,2,0:T(8,128)(4,1)S(1)}) fusion(f32[1,128,8]{1,2,0:T(8,128)} %param.7, s32[1,128,8]{1,2,0:T(8,128)} %param.6), kind=kLoop, calls=%fused_computation.19 | loop fusion | flops 2944 | bytes 9728 | tf_op jit(solution)/shard_map/reduce_sum | solution.py:27
  0.7 0.1 copy.8
  0.9 0.2 reduce-window.8
  1.0 0.1 add_reduce_fusion
  1.1 1.4 %convolution_convert_fusion.1 = bf16[8,3584]{1,0:T(8,128)(2,1)S(1)} fusion(s32[128]{0:T(128)S(1)} %add_reduce_fusion, pred[128]{0:T(512)(128)(4,1)S(1)} %reduce_or.18, bf16[1,128,3584]{2,1,0:T(8,128)(2,1)} %param.5), kind=kOutput, calls=%fused_computation.4 | convolution fusion | flops 7370752 | bytes 975488 | tf_op jit(solution)/shard_map/dot_general | solution.py:31
  2.5 0.7 %broadcast_in_dim.9 = bf16[4,8,3584]{2,1,0:T(8,128)(2,1)} broadcast(bf16[8,3584]{1,0:T(8,128)(2,1)S(1)} %convolution_convert_fusion.1), dimensions={1,2} | broadcast | bytes 286720 | tf_op jit(solution)/shard_map/broadcast_in_dim | solution.py:34
  3.3 5.2 %all-to-all-start = ((bf16[4,8,3584]{2,1,0:T(8,128)(2,1)}), bf16[4,8,3584]{2,1,0:T(8,128)(2,1)S(1)}, u32[]{:S(2)}, u32[]{:S(2)}) async-start(bf16[4,8,3584]{2,1,0:T(8,128)(2,1)} %broadcast_in_dim.9), calls=%async_computation | async-start | bytes 458752 | tf_op jit(solution)/shard_map/all_to_all | solution.py:35
  8.5 0.0 collective-permute-start
  8.5 0.1 select_reduce_fusion.2
  8.6 5.2 %all-to-all-done = bf16[4,8,3584]{2,1,0:T(8,128)(2,1)S(1)} async-done(((bf16[4,8,3584]{2,1,0:T(8,128)(2,1)}), bf16[4,8,3584]{2,1,0:T(8,128)(2,1)S(1)}, u32[]{:S(2)}, u32[]{:S(2)}) %all-to-all-start) | async-done | bytes 229408 | tf_op jit(solution)/shard_map/all_to_all | solution.py:35
  13.7 0.0 copy-start
  13.7 4.6 %fusion = f32[32,1024]{1,0:T(8,128)S(1)} fusion(bf16[1,3584,1024]{2,1,0:T(8,128)(2,1)} %param.8, bf16[4,8,3584]{2,1,0:T(8,128)(2,1)S(1)} %all-to-all-done), kind=kOutput, calls=%fused_computation | convolution fusion | flops 234881024 | bytes 7700480 | tf_op jit(solution)/shard_map/dot_general | solution.py:37
  18.3 0.0 copy-done
  18.3 1.4 %fusion.2 = bf16[4,8,3584]{2,1,0:T(8,128)(2,1)} fusion(bf16[1,512,3584]{2,1,0:T(8,128)(2,1)S(1)} %copy-done, f32[32,1024]{1,0:T(8,128)S(1)} %fusion), kind=kOutput, calls=%fused_computation.3 | convolution fusion | flops 117653504 | bytes 4030464 | tf_op jit(solution)/shard_map/dot_general | solution.py:39
  19.8 3.4 %all-to-all-start.1 = ((bf16[4,8,3584]{2,1,0:T(8,128)(2,1)}), bf16[4,8,3584]{2,1,0:T(8,128)(2,1)S(1)}, u32[]{:S(2)}, u32[]{:S(2)}) async-start(bf16[4,8,3584]{2,1,0:T(8,128)(2,1)} %fusion.2), calls=%async_computation.1 | async-start | bytes 458752 | tf_op jit(solution)/shard_map/all_to_all | solution.py:41
  23.2 0.1 fusion.13
  23.3 0.1 select_reduce_fusion
  23.4 5.0 %all-to-all-done.1 = bf16[4,8,3584]{2,1,0:T(8,128)(2,1)S(1)} async-done(((bf16[4,8,3584]{2,1,0:T(8,128)(2,1)}), bf16[4,8,3584]{2,1,0:T(8,128)(2,1)S(1)}, u32[]{:S(2)}, u32[]{:S(2)}) %all-to-all-start.1) | async-done | bytes 229408 | tf_op jit(solution)/shard_map/all_to_all | solution.py:41
  28.4 0.1 multiply_convert_fusion
  28.5 0.0 collective-permute-start.2
  28.6 1.7 %collective-permute-start.1 = (s32[8]{0:T(128)S(1)}, s32[8]{0:T(128)S(1)}, u32[]{:S(2)}, u32[]{:S(2)}) collective-permute-start(s32[8]{0:T(128)S(1)} %multiply_add_fusion), channel_id=1, source_target_pairs={{28,0},{0,4},{4,8},{8,12},{12,16},{16,20},{20,24},{24,28},{29,1},{... | collective-permute-start | bytes 104 | tf_op jit(solution)/shard_map/ppermute | solution.py:12
  30.2 3.8 %collective-permute-done.1 = s32[8]{0:T(128)S(1)} collective-permute-done((s32[8]{0:T(128)S(1)}, s32[8]{0:T(128)S(1)}, u32[]{:S(2)}, u32[]{:S(2)}) %collective-permute-start.1) | collective-permute-done | bytes 64 | tf_op jit(solution)/shard_map/ppermute | solution.py:12
  34.0 0.0 collective-permute-done.2
  34.0 0.0 collective-permute-done
  34.0 1.3 %fusion.4 = bf16[1,128,3584]{2,1,0:T(8,128)(2,1)} fusion(bf16[128,3584]{1,0:T(8,128)(2,1)S(1)} %collective-permute-done, bf16[8,3584]{1,0:T(8,128)(2,1)S(1)} %collective-permute-done.2, s32[8]{0:T(128)S(1)} %collective-permute-done.1), kind=kOutput, calls=%fused_computation.7 | convolution fusion | flops 8717312 | bytes 1892384 | tf_op jit(solution)/shard_map/dot_general | solution.py:55
  (4 shorter events, 0.1 us)
Async XLA Ops:
  3.3 10.5 %all-to-all-start = ((bf16[4,8,3584]{2,1,0:T(8,128)(2,1)}), bf16[4,8,3584]{2,1,0:T(8,128)(2,1)S(1)}, u32[]{:S(2)}, u32[]{:S(2)}) async-start(bf16[4,8,3584]{2,1,0:T(8,128)(2,1)} %broadcast_in_dim.9), calls=%async_computation | async-start | bytes 458752 | tf_op jit(solution)/shard_map/all_to_all | solution.py:35
  8.5 25.6 %collective-permute-start = (bf16[128,3584]{1,0:T(8,128)(2,1)}, bf16[128,3584]{1,0:T(8,128)(2,1)S(1)}, u32[]{:S(2)}, u32[]{:S(2)}) collective-permute-start(bf16[128,3584]{1,0:T(8,128)(2,1)} %bitcast.19), channel_id=1, source_target_pairs={{28,0},{0,4},{4,8},{8,12},{12,16},{16,20},{20,24},{24,28},{29,1},{... | collective-permute-start | bytes 2752520 | tf_op jit(solution)/shard_map/ppermute | solution.py:12
  13.7 4.6 %copy-start = (bf16[1,512,3584]{2,1,0:T(8,128)(2,1)S(1)}, bf16[1,512,3584]{2,1,0:T(8,128)(2,1)}, u32[]{:S(2)}) copy-start(bf16[1,512,3584]{2,1,0:T(8,128)(2,1)} %param.9) | copy-start | bytes 11010052
  19.8 8.6 %all-to-all-start.1 = ((bf16[4,8,3584]{2,1,0:T(8,128)(2,1)}), bf16[4,8,3584]{2,1,0:T(8,128)(2,1)S(1)}, u32[]{:S(2)}, u32[]{:S(2)}) async-start(bf16[4,8,3584]{2,1,0:T(8,128)(2,1)} %fusion.2), calls=%async_computation.1 | async-start | bytes 458752 | tf_op jit(solution)/shard_map/all_to_all | solution.py:41
  28.5 5.5 %collective-permute-start.2 = (bf16[8,3584]{1,0:T(8,128)(2,1)S(1)}, bf16[8,3584]{1,0:T(8,128)(2,1)S(1)}, u32[]{:S(2)}, u32[]{:S(2)}) collective-permute-start(bf16[8,3584]{1,0:T(8,128)(2,1)S(1)} %multiply_convert_fusion), channel_id=1, source_target_pairs={{28,0},{0,4},{4,8},{8,12},{12,16},{16,20},{20,24},{24,28},{29,1},{... | collective-permute-start | bytes 172040 | tf_op jit(solution)/shard_map/ppermute | solution.py:12
  28.6 5.5 %collective-permute-start.1 = (s32[8]{0:T(128)S(1)}, s32[8]{0:T(128)S(1)}, u32[]{:S(2)}, u32[]{:S(2)}) collective-permute-start(s32[8]{0:T(128)S(1)} %multiply_add_fusion), channel_id=1, source_target_pairs={{28,0},{0,4},{4,8},{8,12},{12,16},{16,20},{20,24},{24,28},{29,1},{... | collective-permute-start | bytes 104 | tf_op jit(solution)/shard_map/ppermute | solution.py:12
where the time goes:
time: 35.7 us; the launch traced here: 35.3 us
  waiting for transfers between devices  14 us (39%)
  starting transfers between devices  10.3 us (29%)
  matrix products  8.71 us (24%)
  other arithmetic  1.48 us (4%)
  local copies, waits for them, and re-layouts  0.84 us (2%)
    all_to_all x1, starting transfers between devices, per_device(): lax.all_to_all(outbound, 'expert', split_axis=0, concat_axis=0, tiled=True)  5.19 us
    all_to_all x1, waiting for transfers between devices, per_device(): lax.all_to_all(outbound, 'expert', split_axis=0, concat_axis=0, tiled=True)  5.16 us
    all_to_all x1, waiting for transfers between devices, per_device(): lax.all_to_all(partials, 'expert', split_axis=0, concat_axis=0, tiled=True)  5.01 us
    dot_general x1, matrix products, per_device(): jnp.dot(flat_rows, gate_up_local, preferred_element_type=jnp.float32)  4.59 us
    ppermute x3, waiting for transfers between devices, from_behind(): return lax.ppermute(block, axis, route)  3.8 us
    all_to_all x1, starting transfers between devices, per_device(): lax.all_to_all(partials, 'expert', split_axis=0, concat_axis=0, tiled=True)  3.39 us
    ppermute x3, starting transfers between devices, from_behind(): return lax.ppermute(block, axis, route)  1.7 us
    dot_general x1, matrix products, per_device(): jnp.dot(hidden, down_local, preferred_element_type=jnp.float32)  1.42 us
  transfers between devices with their start and end apart: 5, of which 3 were waited for; matrix products, arithmetic and copies ran while one was open for 18% of the time, Pallas kernels for 0%

commit v1 on v0

v1 whole, which is shorter than its diff:
```python
import functools

import jax
import jax.numpy as jnp
from jax import lax
from jax.experimental import pallas as pl
from jax.experimental.pallas import tpu as pltpu
from jax.sharding import PartitionSpec as P

CAP = 8
MESH = pl.DeviceIdType.MESH


def pieces_of(width):
    for count in (4, 2):
        if width % (128 * count) == 0:
            return count
    return 1


def kernel(
    stages,
    peers,
    pieces,
    out_pieces,
    acts,
    routing,
    combine_w,
    w_gate_up,
    w_down,
    landed,
    rows_out,
    select_out,
    acts_v,
    route_v,
    mix_v,
    gate_up_v,
    down_v,
    gathered,
    part_send,
    part_recv,
    table_send,
    table_recv,
    load_sem,
    gate_up_sem,
    down_sem,
    stream_sem,
    table_sem,
    gather_send_sem,
    gather_recv_sem,
    part_send_sem,
    part_recv_sem,
    ready_sem,
):
    stage = lax.axis_index("pipe")
    me = lax.axis_index("expert")
    after = lax.rem(stage + 1, stages)
    before = lax.rem(stage + stages - 1, stages)
    width = acts.shape[2]
    tokens = acts.shape[1]
    hid = w_down.shape[1]
    step = width // pieces

    load_route = pltpu.make_async_copy(routing.at[0], route_v, load_sem.at[0])
    load_mix = pltpu.make_async_copy(combine_w.at[0], mix_v, load_sem.at[1])
    load_acts = pltpu.make_async_copy(acts.at[0], acts_v, load_sem.at[2])
    load_route.start()
    load_mix.start()
    load_acts.start()
    gate_up_loads = []
    for p in range(pieces):
        rows = pl.ds(p * step, step)
        load = pltpu.make_async_copy(
            w_gate_up.at[0, rows, :], gate_up_v.at[rows, :], gate_up_sem.at[p]
        )
        load.start()
        gate_up_loads.append(load)
    load_down = pltpu.make_async_copy(w_down.at[0], down_v, down_sem)
    load_down.start()

    barrier = pltpu.get_barrier_semaphore()
    for k in range(1, peers):
        pl.semaphore_signal(
            barrier, inc=1, device_id=(stage, lax.rem(me + k, peers)), device_id_type=MESH
        )
    pl.semaphore_signal(barrier, inc=1, device_id=(before, me), device_id_type=MESH)
    pl.semaphore_signal(barrier, inc=1, device_id=(after, me), device_id_type=MESH)

    load_route.wait()
    load_mix.wait()
    named = route_v[...] == 0
    named_f = named.astype(jnp.float32)
    mix = jnp.where(named, mix_v[...], 0.0)
    chosen = lax.dot_general(
        jnp.ones((CAP, named_f.shape[1]), jnp.float32),
        named_f,
        (((1,), (1,)), ((), ())),
        preferred_element_type=jnp.float32,
    )
    earlier = (
        lax.broadcasted_iota(jnp.int32, (tokens, tokens), 0)
        <= lax.broadcasted_iota(jnp.int32, (tokens, tokens), 1)
    ).astype(jnp.float32)
    count = jnp.dot(chosen, earlier, preferred_element_type=jnp.float32)
    slot = lax.broadcasted_iota(jnp.int32, (CAP, tokens), 0).astype(jnp.float32) + 1.0
    select = jnp.where((count == slot) & (chosen > 0.5), 1.0, 0.0)
    slot_mix = jnp.dot(
        select, mix, preferred_element_type=jnp.float32, precision=lax.Precision.HIGHEST
    )
    slot_coeff = jnp.sum(slot_mix, axis=1, keepdims=True)
    table_send[...] = select * slot_coeff
    select_b = select.astype(jnp.bfloat16)

    load_acts.wait()
    for p in range(pieces):
        cols = pl.ds(p * step, step)
        gathered[me, :, cols] = jnp.dot(
            select_b, acts_v[:, cols], preferred_element_type=jnp.float32
        ).astype(jnp.bfloat16)

    pl.semaphore_wait(barrier, peers + 1)

    gathers = []
    for p in range(pieces):
        cols = pl.ds(p * step, step)
        for k in range(1, peers):
            copy = pltpu.make_async_remote_copy(
                src_ref=gathered.at[me, :, cols],
                dst_ref=gathered.at[me, :, cols],
                send_sem=gather_send_sem.at[p, k],
                recv_sem=gather_recv_sem.at[p, me],
                device_id=(stage, lax.rem(me + k, peers)),
                device_id_type=MESH,
            )
            copy.start()
            gathers.append(copy)
    stream = pltpu.make_async_remote_copy(
        src_ref=acts,
        dst_ref=landed,
        send_sem=stream_sem.at[0],
        recv_sem=stream_sem.at[1],
        device_id=(after, me),
        device_id_type=MESH,
    )
    stream.start()
    table = pltpu.make_async_remote_copy(
        src_ref=table_send,
        dst_ref=table_recv,
        send_sem=table_sem.at[0],
        recv_sem=table_sem.at[1],
        device_id=(after, me),
        device_id_type=MESH,
    )
    table.start()
    for k in range(1, peers):
        pl.semaphore_signal(
            ready_sem, inc=1, device_id=(stage, lax.rem(me + k, peers)), device_id_type=MESH
        )

    total = None
    for p in range(pieces):
        cols = pl.ds(p * step, step)
        gate_up_loads[p].wait()
        for k in range(1, peers):
            source = lax.rem(me + k, peers)
            pltpu.make_async_remote_copy(
                src_ref=gathered.at[source, :, cols],
                dst_ref=gathered.at[source, :, cols],
                send_sem=gather_send_sem.at[p, k],
                recv_sem=gather_recv_sem.at[p, source],
                device_id=(stage, source),
                device_id_type=MESH,
            ).wait_recv()
        rows = (
            gathered[:, :, cols]
            .astype(jnp.float32)
            .reshape(peers * CAP, step)
            .astype(jnp.bfloat16)
        )
        term = jnp.dot(
            rows, gate_up_v[pl.ds(p * step, step), :], preferred_element_type=jnp.float32
        )
        total = term if total is None else total + term
    gate = total[:, :hid]
    up = total[:, hid:]
    hidden = (gate / (1.0 + jnp.exp(-gate)) * up).astype(jnp.bfloat16)

    load_down.wait()
    if peers > 1:
        pl.semaphore_wait(ready_sem, peers - 1)
    out_step = width // out_pieces
    for p in range(out_pieces):
        cols = pl.ds(p * out_step, out_step)
        part = jnp.dot(hidden, down_v[:, cols], preferred_element_type=jnp.float32)
        part_send[:, :, cols] = part.reshape(peers, CAP, out_step).astype(jnp.bfloat16)
        for k in range(peers):
            owner = lax.rem(me + k, peers)
            pltpu.make_async_remote_copy(
                src_ref=part_send.at[owner, :, cols],
                dst_ref=part_recv.at[me, :, cols],
                send_sem=part_send_sem.at[k],
                recv_sem=part_recv_sem.at[me],
                device_id=(after, owner),
                device_id_type=MESH,
            ).start()

    table.wait()
    coeff_in = jnp.sum(table_recv[...], axis=1, keepdims=True)
    select_out[...] = jnp.where(table_recv[...] != 0.0, 1.0, 0.0).astype(jnp.bfloat16)
    for copy in gathers:
        copy.wait_send()
    stream.wait()
    for k in range(peers):
        source = lax.rem(me + k, peers)
        pltpu.make_async_remote_copy(
            src_ref=part_send.at[source],
            dst_ref=part_recv.at[source],
            send_sem=part_send_sem.at[k],
            recv_sem=part_recv_sem.at[source],
            device_id=(after, source),
            device_id_type=MESH,
        ).wait()
    merged = jnp.sum(part_recv[...].astype(jnp.float32), axis=0)
    rows_out[...] = (merged * coeff_in).astype(jnp.bfloat16)


def per_device(stages, peers, acts, routing, combine_w, w_gate_up, w_down):
    _, tokens, width = acts.shape
    hid = w_down.shape[1]
    pieces = pieces_of(width)
    out_pieces = pieces
    anywhere = pl.BlockSpec(memory_space=pl.ANY)
    in_vmem = pl.BlockSpec(memory_space=pltpu.VMEM)
    dma = pltpu.SemaphoreType.DMA
    landed, rows, select = pl.pallas_call(
        functools.partial(kernel, stages, peers, pieces, out_pieces),
        out_shape=(
            jax.ShapeDtypeStruct(acts.shape, acts.dtype),
            jax.ShapeDtypeStruct((CAP, width), jnp.bfloat16),
            jax.ShapeDtypeStruct((CAP, tokens), jnp.bfloat16),
        ),
        in_specs=[anywhere] * 5,
        out_specs=(anywhere, in_vmem, in_vmem),
        scratch_shapes=[
            pltpu.VMEM((tokens, width), acts.dtype),
            pltpu.VMEM(routing.shape[1:], routing.dtype),
            pltpu.VMEM(combine_w.shape[1:], combine_w.dtype),
            pltpu.VMEM(w_gate_up.shape[1:], w_gate_up.dtype),
            pltpu.VMEM(w_down.shape[1:], w_down.dtype),
            pltpu.VMEM((peers, CAP, width), jnp.bfloat16),
            pltpu.VMEM((peers, CAP, width), jnp.bfloat16),
            pltpu.VMEM((peers, CAP, width), jnp.bfloat16),
            pltpu.VMEM((CAP, tokens), jnp.float32),
            pltpu.VMEM((CAP, tokens), jnp.float32),
            dma((3,)),
            dma((pieces,)),
            dma,
            dma((2,)),
            dma((2,)),
            dma((pieces, peers)),
            dma((pieces, peers)),
            dma((peers,)),
            dma((peers,)),
            pltpu.SemaphoreType.REGULAR,
        ],
        compiler_params=pltpu.CompilerParams(collective_id=0, has_side_effects=True),
        name="relay_tick",
    )(acts, routing, combine_w, w_gate_up, w_down)
    layer = lax.dot_general(
        select, rows, (((0,), (0,)), ((), ())), preferred_element_type=jnp.float32
    )
    return (landed[0].astype(jnp.float32) + layer).astype(acts.dtype)[None]


def solution(mesh):
    return jax.shard_map(
        functools.partial(per_device, mesh.shape["pipe"], mesh.shape["expert"]),
        mesh=mesh,
        in_specs=(
            P("pipe", "expert", None),
            P("pipe", "expert", None),
            P("pipe", "expert", None),
            P("pipe", None, "expert"),
            P("pipe", "expert", None),
        ),
        out_specs=P("pipe", "expert", None),
        check_vma=False,
    )
```

time: 35.7 us -> 29.9 us (0.84)
  Pallas kernels: 0 us -> 24.2 us
  waiting for transfers between devices: 14 us -> 0 us
  starting transfers between devices: 10.3 us -> 0 us
  matrix products: 8.71 us -> 2.59 us
  local copies, waits for them, and re-layouts: 0.84 us -> 2.83 us
  other arithmetic: 1.48 us -> 0 us
    pallas_call x0 -> x1, Pallas kernels: none -> 24.2 us  [per_device(): pl.pallas_call(functools.partial(kernel, stages, peers, pieces, out_piece...]
    all_to_all x2 -> x0, waiting for transfers between devices: 10.2 us -> none  [the longest x1 5.16 us: per_device(): lax.all_to_all(outbound, 'expert', split_axis=0, concat_axis=0, tiled=True)]
    all_to_all x2 -> x0, starting transfers between devices: 8.58 us -> none  [the longest x1 5.19 us: per_device(): lax.all_to_all(outbound, 'expert', split_axis=0, concat_axis=0, tiled=True)]
    dot_general x4 -> x1, matrix products: 8.71 us -> 2.59 us  [per_device(): lax.dot_general(select, rows, (((0,), (0,)), ((), ())), preferred_element...]
    ppermute x3 -> x0, waiting for transfers between devices: 3.8 us -> none  [from_behind(): return lax.ppermute(block, axis, route)]
    unnamed x2, local copies, waits for them, and re-layouts: 0.01 us -> 2.83 us
    ppermute x3 -> x0, starting transfers between devices: 1.7 us -> none  [from_behind(): return lax.ppermute(block, axis, route)]
    reduce_sum x4 -> x0, other arithmetic: 0.98 us -> none  [the longest x1 0.72 us: per_device(): coefficient = jnp.sum(jnp.where(names_zero, mix_weights, 0.0), axis=1)]
  transfers between devices with their start and end apart: 5 -> 0, of which waited for: 3 -> 0; matrix products, arithmetic and copies ran while one was open for 18% -> 0% of each run, Pallas kernels for 0% -> 0%
where the time goes in v1:
time: 29.9 us; the launch traced here: 29.7 us
  Pallas kernels  24.2 us (81%)
  local copies, waits for them, and re-layouts  2.83 us (9%)
  matrix products  2.59 us (9%)
    pallas_call x1, Pallas kernels, per_device(): pl.pallas_call(functools.partial(kernel, stages, peers, pieces, out_piece...  24.2 us
    unnamed x2, local copies, waits for them, and re-layouts  2.83 us
    dot_general x1, matrix products, per_device(): lax.dot_general(select, rows, (((0,), (0,)), ((), ())), preferred_element...  2.59 us

profile of v1, /device:TPU:0, one launch (start us, length us, event | category | flops | bytes accessed | tf_op | source)
XLA Modules:
  0.0 29.7 jit_solution(8859504527000854997)
XLA Ops:
  0.0 1.4 %copy.6.routing = s32[1,128,8]{2,1,0:T(8,128)} copy(s32[1,128,8]{1,2,0:T(8,128)} %param.6) | data formatting | bytes 8192 | tf_op args[1]
  1.4 1.4 %copy.7.combine_w = f32[1,128,8]{2,1,0:T(8,128)} copy(f32[1,128,8]{1,2,0:T(8,128)} %param.7) | data formatting | bytes 8192 | tf_op args[2]
  2.8 24.2 %relay_tick.1 = (bf16[1,128,3584]{2,1,0:T(8,128)(2,1)}, bf16[8,3584]{1,0:T(8,128)(2,1)}, bf16[8,128]{1,0:T(8,128)(2,1)}) custom-call(bf16[1,128,3584]{2,1,0:T(8,128)(2,1)} %acts.1, s32[1,128,8]{2,1,0:T(8,128)} %copy.6.routing, f32[1,128,8]{2,1,0:T(8,128)} %copy.7.combine_w, bf16[1,3584,1024]{2,1,0:T(8,128)(2,1)} %w_gate_up.1, bf16[1,512,3584]{2,1,0:T(8,128)(2,1)} %w_down.1), custom_call_target="tpu_custom_call" | custom-call | tf_op jit(solution)/shard_map/relay_tick/pallas_call | solution.py:235
  27.1 2.6 %fusion.1 = bf16[1,128,3584]{2,1,0:T(8,128)(2,1)} fusion(bf16[8,128]{1,0:T(8,128)(2,1)} %get-tuple-element.9, bf16[8,3584]{1,0:T(8,128)(2,1)} %get-tuple-element.10, bf16[1,128,3584]{2,1,0:T(8,128)(2,1)} %get-tuple-element.8), kind=kOutput, calls=%fused_computation.2 | convolution fusion | flops 8716288 | bytes 1894400 | tf_op jit(solution)/shard_map/dot_general | solution.py:269

commit v2 on v1

--- a/solution.py
+++ b/solution.py
@@ -28,9 +28,8 @@
     combine_w,
     w_gate_up,
     w_down,
+    out,
     landed,
-    rows_out,
-    select_out,
     acts_v,
     route_v,
     mix_v,
@@ -61,6 +60,14 @@
     hid = w_down.shape[1]
     step = width // pieces
 
+    barrier = pltpu.get_barrier_semaphore()
+    for k in range(1, peers):
+        pl.semaphore_signal(
+            barrier, inc=1, device_id=(stage, lax.rem(me + k, peers)), device_id_type=MESH
+        )
+    pl.semaphore_signal(barrier, inc=1, device_id=(before, me), device_id_type=MESH)
+    pl.semaphore_signal(barrier, inc=1, device_id=(after, me), device_id_type=MESH)
+
     load_route = pltpu.make_async_copy(routing.at[0], route_v, load_sem.at[0])
     load_mix = pltpu.make_async_copy(combine_w.at[0], mix_v, load_sem.at[1])
     load_acts = pltpu.make_async_copy(acts.at[0], acts_v, load_sem.at[2])
@@ -78,51 +85,41 @@
     load_down = pltpu.make_async_copy(w_down.at[0], down_v, down_sem)
     load_down.start()
 
-    barrier = pltpu.get_barrier_semaphore()
-    for k in range(1, peers):
-        pl.semaphore_signal(
-            barrier, inc=1, device_id=(stage, lax.rem(me + k, peers)), device_id_type=MESH
-        )
-    pl.semaphore_signal(barrier, inc=1, device_id=(before, me), device_id_type=MESH)
-    pl.semaphore_signal(barrier, inc=1, device_id=(after, me), device_id_type=MESH)
-
     load_route.wait()
     load_mix.wait()
     named = route_v[...] == 0
-    named_f = named.astype(jnp.float32)
-    mix = jnp.where(named, mix_v[...], 0.0)
-    chosen = lax.dot_general(
-        jnp.ones((CAP, named_f.shape[1]), jnp.float32),
-        named_f,
-        (((1,), (1,)), ((), ())),
-        preferred_element_type=jnp.float32,
-    )
+    chosen = jnp.max(jnp.where(named, 1.0, 0.0), axis=0, keepdims=True)
+    coefficient = jnp.sum(jnp.where(named, mix_v[...], 0.0), axis=0, keepdims=True)
     earlier = (
         lax.broadcasted_iota(jnp.int32, (tokens, tokens), 0)
         <= lax.broadcasted_iota(jnp.int32, (tokens, tokens), 1)
     ).astype(jnp.float32)
-    count = jnp.dot(chosen, earlier, preferred_element_type=jnp.float32)
+    count = jnp.dot(
+        jnp.broadcast_to(chosen, (CAP, tokens)), earlier, preferred_element_type=jnp.float32
+    )
     slot = lax.broadcasted_iota(jnp.int32, (CAP, tokens), 0).astype(jnp.float32) + 1.0
     select = jnp.where((count == slot) & (chosen > 0.5), 1.0, 0.0)
-    slot_mix = jnp.dot(
-        select, mix, preferred_element_type=jnp.float32, precision=lax.Precision.HIGHEST
-    )
-    slot_coeff = jnp.sum(slot_mix, axis=1, keepdims=True)
-    table_send[...] = select * slot_coeff
+    table_send[...] = select * coefficient
     select_b = select.astype(jnp.bfloat16)
 
+    pl.semaphore_wait(barrier, peers + 1)
+    stream = pltpu.make_async_remote_copy(
+        src_ref=acts,
+        dst_ref=landed,
+        send_sem=stream_sem.at[0],
+        recv_sem=stream_sem.at[1],
+        device_id=(after, me),
+        device_id_type=MESH,
+    )
+    stream.start()
+
     load_acts.wait()
+    gathers = []
     for p in range(pieces):
         cols = pl.ds(p * step, step)
         gathered[me, :, cols] = jnp.dot(
             select_b, acts_v[:, cols], preferred_element_type=jnp.float32
         ).astype(jnp.bfloat16)
-
-    pl.semaphore_wait(barrier, peers + 1)
-
-    gathers = []
-    for p in range(pieces):
-        cols = pl.ds(p * step, step)
         for k in range(1, peers):
             copy = pltpu.make_async_remote_copy(
                 src_ref=gathered.at[me, :, cols],
@@ -134,15 +131,6 @@
             )
             copy.start()
             gathers.append(copy)
-    stream = pltpu.make_async_remote_copy(
-        src_ref=acts,
-        dst_ref=landed,
-        send_sem=stream_sem.at[0],
-        recv_sem=stream_sem.at[1],
-        device_id=(after, me),
-        device_id_type=MESH,
-    )
-    stream.start()
     table = pltpu.make_async_remote_copy(
         src_ref=table_send,
         dst_ref=table_recv,
@@ -206,7 +194,7 @@
 
     table.wait()
     coeff_in = jnp.sum(table_recv[...], axis=1, keepdims=True)
-    select_out[...] = jnp.where(table_recv[...] != 0.0, 1.0, 0.0).astype(jnp.bfloat16)
+    spread = jnp.where(table_recv[...] != 0.0, 1.0, 0.0).astype(jnp.bfloat16)
     for copy in gathers:
         copy.wait_send()
     stream.wait()
@@ -220,28 +208,32 @@
             device_id=(after, source),
             device_id_type=MESH,
         ).wait()
-    merged = jnp.sum(part_recv[...].astype(jnp.float32), axis=0)
-    rows_out[...] = (merged * coeff_in).astype(jnp.bfloat16)
+    for p in range(out_pieces):
+        cols = pl.ds(p * out_step, out_step)
+        merged = jnp.sum(part_recv[:, :, cols].astype(jnp.float32), axis=0)
+        rows = (merged * coeff_in).astype(jnp.bfloat16)
+        layer = lax.dot_general(
+            spread, rows, (((0,), (0,)), ((), ())), preferred_element_type=jnp.float32
+        )
+        out[0, :, cols] = (landed[0, :, cols].astype(jnp.float32) + layer).astype(out.dtype)
 
 
 def per_device(stages, peers, acts, routing, combine_w, w_gate_up, w_down):
     _, tokens, width = acts.shape
-    hid = w_down.shape[1]
+    routing = jnp.swapaxes(routing, 1, 2)
+    combine_w = jnp.swapaxes(combine_w, 1, 2)
     pieces = pieces_of(width)
     out_pieces = pieces
     anywhere = pl.BlockSpec(memory_space=pl.ANY)
     in_vmem = pl.BlockSpec(memory_space=pltpu.VMEM)
     dma = pltpu.SemaphoreType.DMA
-    landed, rows, select = pl.pallas_call(
+    return pl.pallas_call(
         functools.partial(kernel, stages, peers, pieces, out_pieces),
-        out_shape=(
-            jax.ShapeDtypeStruct(acts.shape, acts.dtype),
-            jax.ShapeDtypeStruct((CAP, width), jnp.bfloat16),
-            jax.ShapeDtypeStruct((CAP, tokens), jnp.bfloat16),
-        ),
+        out_shape=pltpu.VMEM(acts.shape, acts.dtype),
         in_specs=[anywhere] * 5,
-        out_specs=(anywhere, in_vmem, in_vmem),
+        out_specs=in_vmem,
         scratch_shapes=[
+            pltpu.VMEM(acts.shape, acts.dtype),
             pltpu.VMEM((tokens, width), acts.dtype),
             pltpu.VMEM(routing.shape[1:], routing.dtype),
             pltpu.VMEM(combine_w.shape[1:], combine_w.dtype),
@@ -266,10 +258,6 @@
         compiler_params=pltpu.CompilerParams(collective_id=0, has_side_effects=True),
         name="relay_tick",
     )(acts, routing, combine_w, w_gate_up, w_down)
-    layer = lax.dot_general(
-        select, rows, (((0,), (0,)), ((), ())), preferred_element_type=jnp.float32
-    )
-    return (landed[0].astype(jnp.float32) + layer).astype(acts.dtype)[None]
 
 
 def solution(mesh):

time: 29.9 us -> 23.8 us (0.80)
  matrix products: 2.59 us -> 0 us
  local copies, waits for them, and re-layouts: 2.83 us -> 0.93 us
  Pallas kernels: 24.2 us -> 22.7 us
    dot_general x1 -> x0, matrix products: 2.59 us -> none  [per_device(): lax.dot_general(select, rows, (((0,), (0,)), ((), ())), preferred_element...]
    unnamed x2 -> x1, local copies, waits for them, and re-layouts: 2.83 us -> 0.93 us
    pallas_call x1, Pallas kernels: 24.2 us -> 22.7 us  [per_device(): pl.pallas_call(functools.partial(kernel, stages, peers, pieces, out_piece...]
where the time goes in v2:
time: 23.8 us; the launch traced here: 23.6 us
  Pallas kernels  22.7 us (95%)
  local copies, waits for them, and re-layouts  0.93 us (4%)
    pallas_call x1, Pallas kernels, per_device(): pl.pallas_call(functools.partial(kernel, stages, peers, pieces, out_piece...  22.7 us
    unnamed x1, local copies, waits for them, and re-layouts  0.93 us

profile of v2, /device:TPU:0, one launch (start us, length us, event | category | flops | bytes accessed | tf_op | source)
XLA Modules:
  0.0 23.6 jit_solution(6760064519893299726)
XLA Ops:
  0.0 22.7 %relay_tick.1 = bf16[1,128,3584]{2,1,0:T(8,128)(2,1)S(1)} custom-call(bf16[1,128,3584]{2,1,0:T(8,128)(2,1)} %acts.1, s32[1,8,128]{2,1,0:T(8,128)} %bitcast.2, f32[1,8,128]{2,1,0:T(8,128)} %bitcast.3, bf16[1,3584,1024]{2,1,0:T(8,128)(2,1)} %w_gate_up.1, bf16[1,512,3584]{2,1,0:T(8,128)(2,1)} %w_down.1), custom_call_target="tpu_custom_call" | custom-call | tf_op jit(solution)/shard_map/relay_tick/pallas_call | solution.py:230
  22.7 0.9 %copy.7 = bf16[1,128,3584]{2,1,0:T(8,128)(2,1)} copy(bf16[1,128,3584]{2,1,0:T(8,128)(2,1)S(1)} %relay_tick.1) | data formatting | bytes 1835008

commit v3 on v2

--- a/solution.py
+++ b/solution.py
@@ -12,7 +12,7 @@
 
 
 def pieces_of(width):
-    for count in (4, 2):
+    for count in (2,):
         if width % (128 * count) == 0:
             return count
     return 1
@@ -22,7 +22,7 @@
     stages,
     peers,
     pieces,
-    out_pieces,
+    row_pieces,
     acts,
     routing,
     combine_w,
@@ -38,6 +38,8 @@
     gathered,
     part_send,
     part_recv,
+    rows_send,
+    rows_recv,
     table_send,
     table_recv,
     load_sem,
@@ -49,7 +51,7 @@
     gather_recv_sem,
     part_send_sem,
     part_recv_sem,
-    ready_sem,
+    rows_sem,
 ):
     stage = lax.axis_index("pipe")
     me = lax.axis_index("expert")
@@ -59,6 +61,7 @@
     tokens = acts.shape[1]
     hid = w_down.shape[1]
     step = width // pieces
+    row_step = tokens // row_pieces
 
     barrier = pltpu.get_barrier_semaphore()
     for k in range(1, peers):
@@ -84,6 +87,21 @@
         gate_up_loads.append(load)
     load_down = pltpu.make_async_copy(w_down.at[0], down_v, down_sem)
     load_down.start()
+
+    pl.semaphore_wait(barrier, peers + 1)
+    streams = []
+    for p in range(row_pieces):
+        span = pl.ds(p * row_step, row_step)
+        stream = pltpu.make_async_remote_copy(
+            src_ref=acts.at[:, span, :],
+            dst_ref=landed.at[:, span, :],
+            send_sem=stream_sem.at[0, p],
+            recv_sem=stream_sem.at[1, p],
+            device_id=(after, me),
+            device_id_type=MESH,
+        )
+        stream.start()
+        streams.append(stream)
 
     load_route.wait()
     load_mix.wait()
@@ -99,19 +117,9 @@
     )
     slot = lax.broadcasted_iota(jnp.int32, (CAP, tokens), 0).astype(jnp.float32) + 1.0
     select = jnp.where((count == slot) & (chosen > 0.5), 1.0, 0.0)
-    table_send[...] = select * coefficient
+    slot_coeff = jnp.sum(select * coefficient, axis=1, keepdims=True)
     select_b = select.astype(jnp.bfloat16)
-
-    pl.semaphore_wait(barrier, peers + 1)
-    stream = pltpu.make_async_remote_copy(
-        src_ref=acts,
-        dst_ref=landed,
-        send_sem=stream_sem.at[0],
-        recv_sem=stream_sem.at[1],
-        device_id=(after, me),
-        device_id_type=MESH,
-    )
-    stream.start()
+    table_send[...] = select_b
 
     load_acts.wait()
     gathers = []
@@ -140,11 +148,6 @@
         device_id_type=MESH,
     )
     table.start()
-    for k in range(1, peers):
-        pl.semaphore_signal(
-            ready_sem, inc=1, device_id=(stage, lax.rem(me + k, peers)), device_id_type=MESH
-        )
-
     total = None
     for p in range(pieces):
         cols = pl.ds(p * step, step)
@@ -174,48 +177,74 @@
     hidden = (gate / (1.0 + jnp.exp(-gate)) * up).astype(jnp.bfloat16)
 
     load_down.wait()
-    if peers > 1:
-        pl.semaphore_wait(ready_sem, peers - 1)
-    out_step = width // out_pieces
-    for p in range(out_pieces):
-        cols = pl.ds(p * out_step, out_step)
+    for p in range(pieces):
+        cols = pl.ds(p * step, step)
         part = jnp.dot(hidden, down_v[:, cols], preferred_element_type=jnp.float32)
-        part_send[:, :, cols] = part.reshape(peers, CAP, out_step).astype(jnp.bfloat16)
-        for k in range(peers):
+        part_send[:, :, cols] = part.reshape(peers, CAP, step).astype(jnp.bfloat16)
+        for k in range(1, peers):
             owner = lax.rem(me + k, peers)
             pltpu.make_async_remote_copy(
                 src_ref=part_send.at[owner, :, cols],
                 dst_ref=part_recv.at[me, :, cols],
-                send_sem=part_send_sem.at[k],
-                recv_sem=part_recv_sem.at[me],
-                device_id=(after, owner),
+                send_sem=part_send_sem.at[p, k],
+                recv_sem=part_recv_sem.at[p, me],
+                device_id=(stage, owner),
                 device_id_type=MESH,
             ).start()
 
-    table.wait()
-    coeff_in = jnp.sum(table_recv[...], axis=1, keepdims=True)
-    spread = jnp.where(table_recv[...] != 0.0, 1.0, 0.0).astype(jnp.bfloat16)
+    forwards = []
+    for p in range(pieces):
+        cols = pl.ds(p * step, step)
+        merged = part_send[me, :, cols].astype(jnp.float32)
+        for k in range(1, peers):
+            source = lax.rem(me + k, peers)
+            pltpu.make_async_remote_copy(
+                src_ref=part_send.at[source, :, cols],
+                dst_ref=part_recv.at[source, :, cols],
+                send_sem=part_send_sem.at[p, k],
+                recv_sem=part_recv_sem.at[p, source],
+                device_id=(stage, source),
+                device_id_type=MESH,
+            ).wait_recv()
+            merged = merged + part_recv[source, :, cols].astype(jnp.float32)
+        rows_send[:, cols] = (merged * slot_coeff).astype(jnp.bfloat16)
+        forward = pltpu.make_async_remote_copy(
+            src_ref=rows_send.at[:, cols],
+            dst_ref=rows_recv.at[:, cols],
+            send_sem=rows_sem.at[0, p],
+            recv_sem=rows_sem.at[1, p],
+            device_id=(after, me),
+            device_id_type=MESH,
+        )
+        forward.start()
+        forwards.append(forward)
+
     for copy in gathers:
         copy.wait_send()
-    stream.wait()
-    for k in range(peers):
-        source = lax.rem(me + k, peers)
-        pltpu.make_async_remote_copy(
-            src_ref=part_send.at[source],
-            dst_ref=part_recv.at[source],
-            send_sem=part_send_sem.at[k],
-            recv_sem=part_recv_sem.at[source],
-            device_id=(after, source),
-            device_id_type=MESH,
-        ).wait()
-    for p in range(out_pieces):
-        cols = pl.ds(p * out_step, out_step)
-        merged = jnp.sum(part_recv[:, :, cols].astype(jnp.float32), axis=0)
-        rows = (merged * coeff_in).astype(jnp.bfloat16)
+    for p in range(pieces):
+        for k in range(1, peers):
+            owner = lax.rem(me + k, peers)
+            pltpu.make_async_remote_copy(
+                src_ref=part_send.at[owner, :, pl.ds(p * step, step)],
+                dst_ref=part_recv.at[me, :, pl.ds(p * step, step)],
+                send_sem=part_send_sem.at[p, k],
+                recv_sem=part_recv_sem.at[p, me],
+                device_id=(stage, owner),
+                device_id_type=MESH,
+            ).wait_send()
+    table.wait()
+    for forward in forwards:
+        forward.wait()
+    for p in range(row_pieces):
+        span = pl.ds(p * row_step, row_step)
+        streams[p].wait()
         layer = lax.dot_general(
-            spread, rows, (((0,), (0,)), ((), ())), preferred_element_type=jnp.float32
-        )
-        out[0, :, cols] = (landed[0, :, cols].astype(jnp.float32) + layer).astype(out.dtype)
+            table_recv[:, span],
+            rows_recv[...],
+            (((0,), (0,)), ((), ())),
+            preferred_element_type=jnp.float32,
+        )
+        out[0, span, :] = (landed[0, span, :].astype(jnp.float32) + layer).astype(out.dtype)
 
 
 def per_device(stages, peers, acts, routing, combine_w, w_gate_up, w_down):
@@ -223,12 +252,12 @@
     routing = jnp.swapaxes(routing, 1, 2)
     combine_w = jnp.swapaxes(combine_w, 1, 2)
     pieces = pieces_of(width)
-    out_pieces = pieces
+    row_pieces = 1
     anywhere = pl.BlockSpec(memory_space=pl.ANY)
     in_vmem = pl.BlockSpec(memory_space=pltpu.VMEM)
     dma = pltpu.SemaphoreType.DMA
     return pl.pallas_call(
-        functools.partial(kernel, stages, peers, pieces, out_pieces),
+        functools.partial(kernel, stages, peers, pieces, row_pieces),
         out_shape=pltpu.VMEM(acts.shape, acts.dtype),
         in_specs=[anywhere] * 5,
         out_specs=in_vmem,
@@ -242,18 +271,20 @@
             pltpu.VMEM((peers, CAP, width), jnp.bfloat16),
             pltpu.VMEM((peers, CAP, width), jnp.bfloat16),
             pltpu.VMEM((peers, CAP, width), jnp.bfloat16),
-            pltpu.VMEM((CAP, tokens), jnp.float32),
-            pltpu.VMEM((CAP, tokens), jnp.float32),
+            pltpu.VMEM((CAP, width), jnp.bfloat16),
+            pltpu.VMEM((CAP, width), jnp.bfloat16),
+            pltpu.VMEM((CAP, tokens), jnp.bfloat16),
+            pltpu.VMEM((CAP, tokens), jnp.bfloat16),
             dma((3,)),
             dma((pieces,)),
             dma,
-            dma((2,)),
+            dma((2, row_pieces)),
             dma((2,)),
             dma((pieces, peers)),
             dma((pieces, peers)),
-            dma((peers,)),
-            dma((peers,)),
-            pltpu.SemaphoreType.REGULAR,
+            dma((pieces, peers)),
+            dma((pieces, peers)),
+            dma((2, pieces)),
         ],
         compiler_params=pltpu.CompilerParams(collective_id=0, has_side_effects=True),
         name="relay_tick",

time: 23.8 us -> 20.5 us (0.86)
  Pallas kernels: 22.7 us -> 19.4 us
    pallas_call x1, Pallas kernels: 22.7 us -> 19.4 us  [per_device(): pl.pallas_call(functools.partial(kernel, stages, peers, pieces, row_piece...]
where the time goes in v3:
time: 20.5 us; the launch traced here: 20.4 us
  Pallas kernels  19.4 us (95%)
  local copies, waits for them, and re-layouts  0.93 us (5%)
    pallas_call x1, Pallas kernels, per_device(): pl.pallas_call(functools.partial(kernel, stages, peers, pieces, row_piece...  19.4 us
    unnamed x1, local copies, waits for them, and re-layouts  0.93 us

profile of v3, /device:TPU:0, one launch (start us, length us, event | category | flops | bytes accessed | tf_op | source)
XLA Modules:
  0.0 20.4 jit_solution(10684944298838907755)
XLA Ops:
  0.0 19.4 %relay_tick.1 = bf16[1,128,3584]{2,1,0:T(8,128)(2,1)S(1)} custom-call(bf16[1,128,3584]{2,1,0:T(8,128)(2,1)} %acts.1, s32[1,8,128]{2,1,0:T(8,128)} %bitcast.2, f32[1,8,128]{2,1,0:T(8,128)} %bitcast.3, bf16[1,3584,1024]{2,1,0:T(8,128)(2,1)} %w_gate_up.1, bf16[1,512,3584]{2,1,0:T(8,128)(2,1)} %w_down.1), custom_call_target="tpu_custom_call" | custom-call | tf_op jit(solution)/shard_map/relay_tick/pallas_call | solution.py:259
  19.5 0.9 %copy.7 = bf16[1,128,3584]{2,1,0:T(8,128)(2,1)} copy(bf16[1,128,3584]{2,1,0:T(8,128)(2,1)S(1)} %relay_tick.1) | data formatting | bytes 1835008

commit v4 on v3

--- a/solution.py
+++ b/solution.py
@@ -9,13 +9,6 @@
 
 CAP = 8
 MESH = pl.DeviceIdType.MESH
-
-
-def pieces_of(width):
-    for count in (2,):
-        if width % (128 * count) == 0:
-            return count
-    return 1
 
 
 def kernel(
@@ -40,13 +33,10 @@
     part_recv,
     rows_send,
     rows_recv,
-    table_send,
-    table_recv,
     load_sem,
     gate_up_sem,
     down_sem,
     stream_sem,
-    table_sem,
     gather_send_sem,
     gather_recv_sem,
     part_send_sem,
@@ -119,7 +109,7 @@
     select = jnp.where((count == slot) & (chosen > 0.5), 1.0, 0.0)
     slot_coeff = jnp.sum(select * coefficient, axis=1, keepdims=True)
     select_b = select.astype(jnp.bfloat16)
-    table_send[...] = select_b
+    rows_send[:, pl.ds(width, tokens)] = select_b
 
     load_acts.wait()
     gathers = []
@@ -139,15 +129,6 @@
             )
             copy.start()
             gathers.append(copy)
-    table = pltpu.make_async_remote_copy(
-        src_ref=table_send,
-        dst_ref=table_recv,
-        send_sem=table_sem.at[0],
-        recv_sem=table_sem.at[1],
-        device_id=(after, me),
-        device_id_type=MESH,
-    )
-    table.start()
     total = None
     for p in range(pieces):
         cols = pl.ds(p * step, step)
@@ -192,7 +173,6 @@
                 device_id_type=MESH,
             ).start()
 
-    forwards = []
     for p in range(pieces):
         cols = pl.ds(p * step, step)
         merged = part_send[me, :, cols].astype(jnp.float32)
@@ -208,16 +188,15 @@
             ).wait_recv()
             merged = merged + part_recv[source, :, cols].astype(jnp.float32)
         rows_send[:, cols] = (merged * slot_coeff).astype(jnp.bfloat16)
-        forward = pltpu.make_async_remote_copy(
-            src_ref=rows_send.at[:, cols],
-            dst_ref=rows_recv.at[:, cols],
-            send_sem=rows_sem.at[0, p],
-            recv_sem=rows_sem.at[1, p],
-            device_id=(after, me),
-            device_id_type=MESH,
-        )
-        forward.start()
-        forwards.append(forward)
+    forward = pltpu.make_async_remote_copy(
+        src_ref=rows_send,
+        dst_ref=rows_recv,
+        send_sem=rows_sem.at[0],
+        recv_sem=rows_sem.at[1],
+        device_id=(after, me),
+        device_id_type=MESH,
+    )
+    forward.start()
 
     for copy in gathers:
         copy.wait_send()
@@ -232,15 +211,13 @@
                 device_id=(stage, owner),
                 device_id_type=MESH,
             ).wait_send()
-    table.wait()
-    for forward in forwards:
-        forward.wait()
+    forward.wait()
     for p in range(row_pieces):
         span = pl.ds(p * row_step, row_step)
         streams[p].wait()
         layer = lax.dot_general(
-            table_recv[:, span],
-            rows_recv[...],
+            rows_recv[:, pl.ds(width + p * row_step, row_step)],
+            rows_recv[:, pl.ds(0, width)],
             (((0,), (0,)), ((), ())),
             preferred_element_type=jnp.float32,
         )
@@ -251,7 +228,7 @@
     _, tokens, width = acts.shape
     routing = jnp.swapaxes(routing, 1, 2)
     combine_w = jnp.swapaxes(combine_w, 1, 2)
-    pieces = pieces_of(width)
+    pieces = 1
     row_pieces = 1
     anywhere = pl.BlockSpec(memory_space=pl.ANY)
     in_vmem = pl.BlockSpec(memory_space=pltpu.VMEM)
@@ -271,20 +248,17 @@
             pltpu.VMEM((peers, CAP, width), jnp.bfloat16),
             pltpu.VMEM((peers, CAP, width), jnp.bfloat16),
             pltpu.VMEM((peers, CAP, width), jnp.bfloat16),
-            pltpu.VMEM((CAP, width), jnp.bfloat16),
-            pltpu.VMEM((CAP, width), jnp.bfloat16),
-            pltpu.VMEM((CAP, tokens), jnp.bfloat16),
-            pltpu.VMEM((CAP, tokens), jnp.bfloat16),
+            pltpu.VMEM((CAP, width + tokens), jnp.bfloat16),
+            pltpu.VMEM((CAP, width + tokens), jnp.bfloat16),
             dma((3,)),
             dma((pieces,)),
             dma,
             dma((2, row_pieces)),
+            dma((pieces, peers)),
+            dma((pieces, peers)),
+            dma((pieces, peers)),
+            dma((pieces, peers)),
             dma((2,)),
-            dma((pieces, peers)),
-            dma((pieces, peers)),
-            dma((pieces, peers)),
-            dma((pieces, peers)),
-            dma((2, pieces)),
         ],
         compiler_params=pltpu.CompilerParams(collective_id=0, has_side_effects=True),
         name="relay_tick",

time: 20.5 us -> 20.3 us (level)
  no operation moved by 1% of the time
where the time goes in v4:
time: 20.3 us; the launch traced here: 20.2 us
  Pallas kernels  19.3 us (95%)
  local copies, waits for them, and re-layouts  0.93 us (5%)
    pallas_call x1, Pallas kernels, per_device(): pl.pallas_call(functools.partial(kernel, stages, peers, pieces, row_piece...  19.3 us
    unnamed x1, local copies, waits for them, and re-layouts  0.93 us

profile of v4, /device:TPU:0, one launch (start us, length us, event | category | flops | bytes accessed | tf_op | source)
XLA Modules:
  0.0 20.2 jit_solution(6642937340357654539)
XLA Ops:
  0.0 19.3 %relay_tick.1 = bf16[1,128,3584]{2,1,0:T(8,128)(2,1)S(1)} custom-call(bf16[1,128,3584]{2,1,0:T(8,128)(2,1)} %acts.1, s32[1,8,128]{2,1,0:T(8,128)} %bitcast.2, f32[1,8,128]{2,1,0:T(8,128)} %bitcast.3, bf16[1,3584,1024]{2,1,0:T(8,128)(2,1)} %w_gate_up.1, bf16[1,512,3584]{2,1,0:T(8,128)(2,1)} %w_down.1), custom_call_target="tpu_custom_call" | custom-call | tf_op jit(solution)/shard_map/relay_tick/pallas_call | solution.py:236
  19.3 0.9 %copy.7 = bf16[1,128,3584]{2,1,0:T(8,128)(2,1)} copy(bf16[1,128,3584]{2,1,0:T(8,128)(2,1)S(1)} %relay_tick.1) | data formatting | bytes 1835008
